TPU v7x, 32 devices: a whole 2x2x4 slice. The times are simulated.
32 devices in a mesh: dp: 4 (over z), freq: 2 (over core), tm: 4 (over y, x).
Axes of the slice: x: 2, y: 2, z: 4, core: 2. Of those that a mesh axis runs over, the one named last changes fastest.
Arguments:
- patches: bfloat16 [1312, 32, 768], P(('freq', 'tm'), 'dp'), may hold values from -6 to 6
- col_counts: int32 [4], replicated, may hold values from 26 to 27, as said below
- norm_gain: bfloat16 [2, 768], replicated, may hold values from 0.099609375 to 1.8984375
- norm_shift: bfloat16 [2, 768], replicated, may hold values from -3 to 3
- joint_proj: bfloat16 [768, 2304], replicated, may hold values from -0.3125 to 0.3125
- proj_bias: bfloat16 [2, 768], replicated, may hold values from -3 to 3
- out_proj: bfloat16 [768, 768], replicated, may hold values from -0.875 to 0.875
- up_proj: bfloat16 [768, 3072], replicated, may hold values from -0.21875 to 0.21875
- up_bias: bfloat16 [3072], replicated, may hold values from -3 to 3
- down_proj: bfloat16 [3072, 768], replicated, may hold values from -0.109375 to 0.109375
- out_bias: bfloat16 [2, 768], replicated, may hold values from -3 to 3
- cotangent: bfloat16 [1312, 32, 768], P(('freq', 'tm'), 'dp'), may hold values from -6 to 6
Outputs:
- output: bfloat16 [1312, 32, 768], P(('freq', 'tm'), 'dp')
- grad_patches: bfloat16 [1312, 32, 768], P(('freq', 'tm'), 'dp')
- grad_norm_gain: float32 [2, 768], P(None, ('freq', 'tm'))
- grad_norm_shift: float32 [2, 768], P(None, ('freq', 'tm'))
- grad_joint_proj: float32 [768, 2304], P(('freq', 'tm'))
- grad_proj_bias: float32 [2, 768], P(None, ('freq', 'tm'))
- grad_out_proj: float32 [768, 768], P(('freq', 'tm'))
- grad_up_proj: float32 [768, 3072], P(('freq', 'tm'))
- grad_up_bias: float32 [3072], P(('freq', 'tm'))
- grad_down_proj: float32 [3072, 768], P(('freq', 'tm'))
- grad_out_bias: float32 [2, 768], P(None, ('freq', 'tm'))
Inputs may be any that keep to these rules, and one draw needn't show every extreme that they name: `col_counts`: each entry is 26 or 27, and both occur in every draw.
All inputs are finite; a program needn't handle non-finite values.
Results may differ from a plain program's by a relative error of at most 0.019.
Values may be sent and summed in bfloat16 or wider, within the bound.
No kernel may reach another device: no remote copies, remote signals or barrier semaphores. Data moves between devices by JAX's collectives and lax.ppermute only.
A program may use at most 448 MiB of HBM per device.

v0:
```python
import math
import jax
import jax.numpy as jnp
from jax import lax
from jax.sharding import PartitionSpec as P

HEADS = 12
DH = 64
FREQ_ROWS = 12
EPS = 1e-06
NEG = -1000000000.0


def live_slots(col_counts, slot_ids, freq_ids, time_ids, freq_rows, cap_cols):
    table = jnp.arange(col_counts.shape[0], dtype=jnp.int32)
    live_cols = jnp.sum(
        jnp.where(time_ids[:, None] == table[None, :], col_counts[None, :], 0), axis=1
    )
    in_grid = slot_ids < freq_rows * cap_cols
    column_live = slot_ids // freq_rows < live_cols
    extra_live = (time_ids == 0) & (freq_ids == 0)
    return jnp.where(in_grid, column_live, extra_live)


def norm_rows(values, gain, shift):
    centered = values - jnp.mean(values, axis=-1, keepdims=True)
    inverse = lax.rsqrt(jnp.mean(centered * centered, axis=-1, keepdims=True) + EPS)
    return centered * inverse * gain + shift


def gelu_exact(values):
    return jax.nn.gelu(values, approximate=False)


def matmul(left, right):
    return jnp.dot(left, right, preferred_element_type=jnp.float32)


def matmul_tn(left, right):
    return lax.dot_general(
        left, right, (((0,), (0,)), ((), ())), preferred_element_type=jnp.float32
    )


def matmul_nt(left, right):
    return lax.dot_general(
        left, right, (((1,), (1,)), ((), ())), preferred_element_type=jnp.float32
    )


def head_pair(array, offset, lane_width, head_size):
    section = lax.dynamic_slice_in_dim(array, offset, lane_width, 2)
    return section.reshape(section.shape[0], section.shape[1], 2, head_size)


def add_lanes(target, addend, offset):
    current = lax.dynamic_slice_in_dim(target, offset, addend.shape[2], 2)
    return lax.dynamic_update_slice_in_dim(target, current + addend, offset, 2)


def pair_probs(query_pair, key_pair, log_pair, mask, scale):
    scores = (
        jnp.einsum("qchd,kchd->chqk", query_pair, key_pair, preferred_element_type=jnp.float32)
        * scale
        + mask
    )
    return jnp.exp(scores - jnp.transpose(log_pair, (1, 2, 0))[..., None])


def per_device(
    patches,
    col_counts,
    norm_gain,
    norm_shift,
    joint_proj,
    proj_bias,
    out_proj,
    up_proj,
    up_bias,
    down_proj,
    out_bias,
    cotangent,
):
    slots, clips, width = patches.shape
    row_count = slots * clips
    lane_width = 2 * DH
    pair_count = HEADS // 2
    scale = 1.0 / math.sqrt(DH)
    freq_size = lax.axis_size("freq")
    time_size = lax.axis_size("tm")
    freq_rows = FREQ_ROWS // freq_size
    cap_cols = (slots - 2) // freq_rows
    key_count = slots * freq_size * time_size
    slot_ids = jnp.arange(slots, dtype=jnp.int32)
    own_live = live_slots(
        col_counts,
        slot_ids,
        jnp.full((slots,), lax.axis_index("freq"), jnp.int32),
        jnp.full((slots,), lax.axis_index("tm"), jnp.int32),
        freq_rows,
        cap_cols,
    )
    key_ids = jnp.arange(key_count, dtype=jnp.int32)
    key_group = key_ids // slots
    key_live = live_slots(
        col_counts,
        key_ids % slots,
        key_group // time_size,
        key_group % time_size,
        freq_rows,
        cap_cols,
    )
    key_mask = jnp.where(key_live, 0.0, NEG).astype(jnp.float32)
    row_live = (
        jnp.broadcast_to(own_live[:, None], (slots, clips))
        .reshape(row_count, 1)
        .astype(jnp.float32)
    )
    gain_full = norm_gain.astype(jnp.float32)
    shift_full = norm_shift.astype(jnp.float32)
    bias_full = proj_bias.astype(jnp.float32)
    outb_full = out_bias.astype(jnp.float32)
    upb_full = up_bias.astype(jnp.float32)
    inputs = patches.reshape(row_count, width).astype(jnp.float32)
    normed1, ln1_back = jax.vjp(norm_rows, inputs, gain_full[0], shift_full[0])
    normed1_low = normed1.astype(jnp.bfloat16)
    joint = matmul(normed1_low, joint_proj)
    query_low = (joint[:, :width] + bias_full[0]).astype(jnp.bfloat16)
    keys_low = joint[:, width : 2 * width].astype(jnp.bfloat16)
    memory_low = (joint[:, 2 * width :] + bias_full[1]).astype(jnp.bfloat16)
    query3 = query_low.reshape(slots, clips, width)
    key_value = jnp.concatenate([keys_low, memory_low], axis=1).reshape(slots, clips, 2 * width)
    all_memory = lax.all_gather(key_value, ("freq", "tm"), axis=0, tiled=True)

    def forward_pair(number, state):
        mixed_acc, log_acc = state
        offset = number * lane_width
        query_pair = head_pair(query3, offset, lane_width, DH)
        key_pair = head_pair(all_memory, offset, lane_width, DH)
        value_pair = head_pair(all_memory, width + offset, lane_width, DH)
        scores = (
            jnp.einsum("qchd,kchd->chqk", query_pair, key_pair, preferred_element_type=jnp.float32)
            * scale
            + key_mask
        )
        highest = jnp.max(scores, axis=-1, keepdims=True)
        exponent = jnp.exp(scores - highest)
        summed = jnp.sum(exponent, axis=-1, keepdims=True)
        attention = (exponent / summed).astype(jnp.bfloat16)
        mixed = jnp.einsum(
            "chqk,kchd->qchd", attention, value_pair, preferred_element_type=jnp.float32
        )
        log_pair = jnp.transpose((highest + jnp.log(summed))[..., 0], (2, 0, 1))
        mixed_acc = lax.dynamic_update_slice_in_dim(
            mixed_acc, mixed.reshape(slots, clips, lane_width), offset, 2
        )
        log_acc = lax.dynamic_update_slice_in_dim(log_acc, log_pair, 2 * number, 2)
        return (mixed_acc, log_acc)

    mixed_full, log_rows = lax.fori_loop(
        0,
        pair_count,
        forward_pair,
        (
            jnp.zeros((slots, clips, width), jnp.float32),
            jnp.zeros((slots, clips, HEADS), jnp.float32),
        ),
    )
    mixed_low = mixed_full.reshape(row_count, width).astype(jnp.bfloat16)
    middle = inputs + matmul(mixed_low, out_proj) + outb_full[0]
    normed2, ln2_back = jax.vjp(norm_rows, middle, gain_full[1], shift_full[1])
    normed2_low = normed2.astype(jnp.bfloat16)
    pre_act = matmul(normed2_low, up_proj) + upb_full
    activated, gelu_back = jax.vjp(gelu_exact, pre_act)
    hidden_low = activated.astype(jnp.bfloat16)
    final = middle + matmul(hidden_low, down_proj) + outb_full[1]
    output = (final * row_live).astype(jnp.bfloat16).reshape(slots, clips, width)
    grad_out_rows = cotangent.reshape(row_count, width).astype(jnp.float32) * row_live
    grad_out_low = grad_out_rows.astype(jnp.bfloat16)
    grad_down_part = matmul_tn(hidden_low, grad_out_low)
    grad_outb_mlp = jnp.sum(grad_out_rows, axis=0)
    grad_hidden = matmul_nt(grad_out_low, down_proj)
    grad_pre_low = gelu_back(grad_hidden)[0].astype(jnp.bfloat16)
    grad_up_part = matmul_tn(normed2_low, grad_pre_low)
    grad_upb_part = jnp.sum(grad_pre_low.astype(jnp.float32), axis=0)
    grad_normed2 = matmul_nt(grad_pre_low, up_proj)
    grad_mid_part, grad_gain_mlp, grad_shift_mlp = ln2_back(grad_normed2)
    grad_middle = grad_out_rows + grad_mid_part
    grad_branch = grad_middle.astype(jnp.bfloat16)
    grad_outp_part = matmul_tn(mixed_low, grad_branch)
    grad_outb_attn = jnp.sum(grad_branch.astype(jnp.float32), axis=0)
    grad_mixed_low = matmul_nt(grad_branch, out_proj).astype(jnp.bfloat16)
    grad_mixed3 = grad_mixed_low.reshape(slots, clips, width)

    def query_side(number):
        offset = number * lane_width
        query_pair = head_pair(query3, offset, lane_width, DH)
        grad_pair = head_pair(grad_mixed3, offset, lane_width, DH)
        key_pair = head_pair(all_memory, offset, lane_width, DH)
        value_pair = head_pair(all_memory, width + offset, lane_width, DH)
        log_pair = lax.dynamic_slice_in_dim(log_rows, 2 * number, 2, 2)
        probability = pair_probs(query_pair, key_pair, log_pair, key_mask, scale)
        grad_probs = jnp.einsum(
            "qchd,kchd->chqk", grad_pair, value_pair, preferred_element_type=jnp.float32
        )
        delta = jnp.sum(probability * grad_probs, axis=-1, keepdims=True)
        grad_scores = (probability * (grad_probs - delta)).astype(jnp.bfloat16)
        grad_query = (
            jnp.einsum("chqk,kchd->qchd", grad_scores, key_pair, preferred_element_type=jnp.float32)
            * scale
        )
        return (
            offset,
            query_pair,
            grad_pair,
            probability,
            grad_scores,
            delta,
            grad_query.reshape(slots, clips, lane_width),
        )

    zero_query = jnp.zeros((slots, clips, width), jnp.float32)

    def backward_pair(number, state):
        grad_query_acc, grad_memory = state
        side = query_side(number)
        offset = side[0]
        grad_keys = (
            jnp.einsum("chqk,qchd->kchd", side[4], side[1], preferred_element_type=jnp.float32)
            * scale
        )
        grad_values = jnp.einsum(
            "chqk,qchd->kchd",
            side[3].astype(jnp.bfloat16),
            side[2],
            preferred_element_type=jnp.float32,
        )
        grad_memory = add_lanes(
            grad_memory, grad_keys.reshape(key_count, clips, lane_width), offset
        )
        grad_memory = add_lanes(
            grad_memory, grad_values.reshape(key_count, clips, lane_width), width + offset
        )
        return (add_lanes(grad_query_acc, side[6], offset), grad_memory)

    grad_query_full, grad_memory_all = lax.fori_loop(
        0,
        pair_count,
        backward_pair,
        (zero_query, jnp.zeros((key_count, clips, 2 * width), jnp.float32)),
    )
    grad_memory_own = lax.psum_scatter(
        grad_memory_all, ("freq", "tm"), scatter_dimension=0, tiled=True
    )
    grad_query_low = grad_query_full.reshape(row_count, width).astype(jnp.bfloat16)
    grad_memory_low = grad_memory_own.reshape(row_count, 2 * width).astype(jnp.bfloat16)
    grad_joint = jnp.concatenate([grad_query_low, grad_memory_low], axis=1)
    grad_joint_part = matmul_tn(normed1_low, grad_joint)
    grad_bias_cols = jnp.stack(
        [
            jnp.sum(grad_query_low.astype(jnp.float32), axis=0),
            jnp.sum(grad_memory_low[:, width:].astype(jnp.float32), axis=0),
        ],
        axis=1,
    )
    grad_normed1 = matmul_nt(grad_joint, joint_proj)
    grad_in_part, grad_gain_attn, grad_shift_attn = ln1_back(grad_normed1)
    grad_patches = (grad_middle + grad_in_part).astype(jnp.bfloat16).reshape(slots, clips, width)
    shares = (
        lax.psum_scatter(
            grad_joint_part.astype(jnp.bfloat16), ("freq", "tm"), scatter_dimension=0, tiled=True
        ).astype(jnp.float32),
        lax.psum_scatter(
            grad_bias_cols.astype(jnp.bfloat16), ("freq", "tm"), scatter_dimension=0, tiled=True
        ).astype(jnp.float32),
        lax.psum_scatter(
            grad_outp_part.astype(jnp.bfloat16), ("freq", "tm"), scatter_dimension=0, tiled=True
        ).astype(jnp.float32),
        lax.psum_scatter(
            grad_outb_attn.astype(jnp.bfloat16), ("freq", "tm"), scatter_dimension=0, tiled=True
        ).astype(jnp.float32),
        lax.psum_scatter(
            grad_gain_attn.astype(jnp.bfloat16), ("freq", "tm"), scatter_dimension=0, tiled=True
        ).astype(jnp.float32),
        lax.psum_scatter(
            grad_shift_attn.astype(jnp.bfloat16), ("freq", "tm"), scatter_dimension=0, tiled=True
        ).astype(jnp.float32),
        lax.psum_scatter(
            grad_up_part.astype(jnp.bfloat16), ("freq", "tm"), scatter_dimension=0, tiled=True
        ).astype(jnp.float32),
        lax.psum_scatter(
            grad_upb_part.astype(jnp.bfloat16), ("freq", "tm"), scatter_dimension=0, tiled=True
        ).astype(jnp.float32),
        lax.psum_scatter(
            grad_down_part.astype(jnp.bfloat16), ("freq", "tm"), scatter_dimension=0, tiled=True
        ).astype(jnp.float32),
        lax.psum_scatter(
            grad_outb_mlp.astype(jnp.bfloat16), ("freq", "tm"), scatter_dimension=0, tiled=True
        ).astype(jnp.float32),
        lax.psum_scatter(
            grad_gain_mlp.astype(jnp.bfloat16), ("freq", "tm"), scatter_dimension=0, tiled=True
        ).astype(jnp.float32),
        lax.psum_scatter(
            grad_shift_mlp.astype(jnp.bfloat16), ("freq", "tm"), scatter_dimension=0, tiled=True
        ).astype(jnp.float32),
    )
    summed_all = (
        lax.psum(shares[0].astype(jnp.bfloat16), "dp").astype(jnp.float32),
        lax.psum(shares[1].astype(jnp.bfloat16), "dp").astype(jnp.float32),
        lax.psum(shares[2].astype(jnp.bfloat16), "dp").astype(jnp.float32),
        lax.psum(shares[3].astype(jnp.bfloat16), "dp").astype(jnp.float32),
        lax.psum(shares[4].astype(jnp.bfloat16), "dp").astype(jnp.float32),
        lax.psum(shares[5].astype(jnp.bfloat16), "dp").astype(jnp.float32),
        lax.psum(shares[6].astype(jnp.bfloat16), "dp").astype(jnp.float32),
        lax.psum(shares[7].astype(jnp.bfloat16), "dp").astype(jnp.float32),
        lax.psum(shares[8].astype(jnp.bfloat16), "dp").astype(jnp.float32),
        lax.psum(shares[9].astype(jnp.bfloat16), "dp").astype(jnp.float32),
        lax.psum(shares[10].astype(jnp.bfloat16), "dp").astype(jnp.float32),
        lax.psum(shares[11].astype(jnp.bfloat16), "dp").astype(jnp.float32),
    )
    attn_summed = summed_all[:6]
    mlp_summed = summed_all[6:]
    grad_norm_gain = jnp.stack([attn_summed[4], mlp_summed[4]])
    grad_norm_shift = jnp.stack([attn_summed[5], mlp_summed[5]])
    grad_out_bias = jnp.stack([attn_summed[3], mlp_summed[3]])
    grad_proj_bias = jnp.transpose(attn_summed[1])
    return (
        output,
        grad_patches,
        grad_norm_gain,
        grad_norm_shift,
        attn_summed[0],
        grad_proj_bias,
        attn_summed[2],
        mlp_summed[0],
        mlp_summed[1],
        mlp_summed[2],
        grad_out_bias,
    )


def solution(mesh):
    return jax.shard_map(
        per_device,
        mesh=mesh,
        in_specs=(
            P(("freq", "tm"), "dp", None),
            P(),
            P(),
            P(),
            P(),
            P(),
            P(),
            P(),
            P(),
            P(),
            P(),
            P(("freq", "tm"), "dp", None),
        ),
        out_specs=(
            P(("freq", "tm"), "dp", None),
            P(("freq", "tm"), "dp", None),
            P(None, ("freq", "tm")),
            P(None, ("freq", "tm")),
            P(("freq", "tm"), None),
            P(None, ("freq", "tm")),
            P(("freq", "tm"), None),
            P(("freq", "tm"), None),
            P(("freq", "tm")),
            P(("freq", "tm"), None),
            P(None, ("freq", "tm")),
        ),
        check_vma=False,
    )
```

profile of v0, /device:TPU:0, one launch (start us, length us, event | category | flops | bytes accessed | tf_op | source)
XLA Modules:
  0.0 1731.1 jit_solution(16705769092683540999)
XLA Ops:
  18.8 6.9 fusion.65
  44.3 144.5 %all-gather.2.cloned.1.call-done = bf16[1312,8,1536]{2,1,0:T(8,128)(2,1)} async-done(((bf16[164,8,1536]{2,1,0:T(8,128)(2,1)}), bf16[1312,8,1536]{2,1,0:T(8,128)(2,1)}) %all-gather.2.cloned.1.call-update) | async-done | bytes 32243728 | tf_op jit(solution)/shard_map/all_gather | solution.py:133
  188.8 42.4 %copy.42 = bf16[1312,8,1536]{0,2,1:T(8,128)(2,1)} copy(bf16[1312,8,1536]{2,1,0:T(8,128)(2,1)} %all-gather.2.cloned.1.call-done) | data formatting | bytes 64487424 | tf_op jit(solution)/shard_map/while | solution.py:160
  231.9 122.6 %while.34 = (s32[]{:T(128)}, bf16[164,8,768]{2,1,0:T(8,128)(2,1)}, f32[164,8,12]{0,2,1:T(8,128)}, bf16[1312,8,1536]{0,2,1:T(8,128)(2,1)}, bf16[164,8,768]{0,2,1:...) while((s32[]{:T(128)}, bf16[164,8,768]{2,1,0:T(8,128)(2,1)}, ...), condition=%wide.region_6.7_spmd, body=%wide.region_3.6_spmd.sunk | while | flops 922637760 | bytes 60295916 | solution.py:160
  360.4 45.8 %multiply_convert_fusion.1 = (bf16[1312,3072]{1,0:T(8,128)(2,1)}, f32[1312,3072]{1,0:T(8,128)}, f32[1312,3072]{1,0:T(8,128)}) fusion(f32[3072]{0:T(1024)S(1)} %copy-done.41, bf16[768,3072]{1,0:T(8,128)(2,1)S(1)} %bitcast.204, f32[1312,768]{1,0:T(8,128)S(1)} %get-tuple-element.504, f32[768]{0:T(1024)S(1)} %copy-done.46, f32[768]{0:T(1024)S(1)} %copy-done.39, ...), kind=kOutput, calls=%fused_computation.34 | convolution fusion | flops 6461841408 | bytes 49082624 | tf_op jit(solution)/shard_map/dot_general | solution.py:36
  406.3 21.5 %fusion.75 = (bf16[3072]{0:T(1024)(128)(2,1)}, bf16[1312,3072]{1,0:T(8,128)(2,1)}) fusion(f32[1312,3072]{1,0:T(8,128)} %get-tuple-element.492, bf16[3072,768]{1,0:T(8,128)(2,1)} %param.25, bf16[164,8,768]{2,1,0:T(8,128)(2,1)} %param.27, f32[1312]{0:T(1024)S(1)} %copy-done.22, f32[1312,3072]{1,0:T(8,128)} %get-tuple-element.505, f32[3072]{0:T(1024)} %convert_element_type.229), kind=kOutput, calls=%fused_computation.178 | convolution fusion | flops 6258299904 | bytes 47062144 | tf_op jit(solution)/shard_map/dot_general | solution.py:46
  427.8 14.1 multiply_reduce_fusion.1
  451.1 21.7 %broadcast_in_dim.96 = f32[1312,8,1536]{0,2,1:T(8,128)} broadcast(f32[]{:T(128)} %constant.301.clone.1), dimensions={} | broadcast | bytes 64487428 | tf_op jit(solution)/shard_map/broadcast_in_dim | solution.py:250
  472.7 478.7 %while.35 = (s32[]{:T(128)}, f32[164,8,768]{2,1,0:T(8,128)}, f32[1312,8,1536]{0,2,1:T(8,128)}, bf16[1312,8,1536]{0,2,1:T(8,128)(2,1)}, bf16[164,8,768]{0,2,1:T(8...) while((s32[]{:T(128)}, f32[164,8,768]{2,1,0:T(8,128)}, ...), condition=%wide.region_14.15_spmd, body=%wide.region_12.14_spmd.sunk | while | flops 2238668288 | bytes 267073456 | solution.py:246
  487.8 7.6 fusion.137
  495.4 11.0 multiply_reduce_fusion.5
  506.5 10.5 multiply_convert_fusion.4
  539.5 7.5 constant_dynamic-update-slice_fusion.10
  567.5 7.6 fusion.137
  575.2 11.0 multiply_reduce_fusion.5
  586.2 10.5 multiply_convert_fusion.4
  619.3 7.5 constant_dynamic-update-slice_fusion.10
  647.3 7.6 fusion.137
  655.0 11.0 multiply_reduce_fusion.5
  666.0 10.5 multiply_convert_fusion.4
  699.2 7.5 constant_dynamic-update-slice_fusion.10
  727.1 7.6 fusion.137
  734.7 11.0 multiply_reduce_fusion.5
  745.8 10.5 multiply_convert_fusion.4
  778.8 7.5 constant_dynamic-update-slice_fusion.10
  806.8 7.6 fusion.137
  814.4 11.0 multiply_reduce_fusion.5
  825.5 10.5 multiply_convert_fusion.4
  858.5 7.5 constant_dynamic-update-slice_fusion.10
  886.4 7.6 fusion.137
  894.1 11.0 multiply_reduce_fusion.5
  905.2 10.5 multiply_convert_fusion.4
  938.3 7.5 constant_dynamic-update-slice_fusion.10
  951.5 67.9 %copy.49 = f32[1312,8,1536]{2,1,0:T(8,128)} copy(f32[1312,8,1536]{0,2,1:T(8,128)} %get-tuple-element.368) | data formatting | bytes 128974848 | tf_op jit(solution)/shard_map/while | solution.py:246
  1024.8 12.6 convolution_convert_fusion.2
  1038.1 15.0 convolution_convert_fusion.1
  1057.5 334.1 %reduce-scatter.9.cloned.1.call-done = f32[164,8,1536]{2,1,0:T(8,128)} async-done(((f32[1312,8,1536]{2,1,0:T(8,128)}), f32[164,8,1536]{2,1,0:T(8,128)}) %reduce-scatter.9.cloned.1.call-update) | async-done | bytes 8060944 | tf_op jit(solution)/shard_map/reduce_scatter | solution.py:252
  1397.5 8.9 convolution_convert_fusion
  1414.3 11.5 fusion.40
  1428.3 11.0 fusion.69
  1445.8 27.6 %all-reduce.7 = (bf16[768]{0:T(1024)(128)(2,1)}, bf16[768]{0:T(1024)(128)(2,1)}, bf16[768]{0:T(1024)(128)(2,1)}, bf16[768]{0:T(1024)(128)(2,1)}, bf16[3072]{0:T(...) all-reduce(bf16[768]{0:T(1024)(128)(2,1)} %get-tuple-element.425, ...), channel_id=4, replica_groups=mesh['dp'=4,'freq'=2,'tm'=4] {'freq','tm'}, use_global_device_ids=true, to_apply=%region_22.23.clone | all-reduce | flops 7680 | bytes 30720
  1474.6 15.7 reduce-scatter.17.cloned.1.call-done
  1490.3 57.2 %reduce-scatter.15.cloned.1.call-done = bf16[96,3072]{1,0:T(8,128)(2,1)} async-done(((bf16[768,3072]{1,0:T(8,128)(2,1)}), bf16[96,3072]{1,0:T(8,128)(2,1)}) %reduce-scatter.15.cloned.1.call-update) | async-done | bytes 589840 | tf_op jit(solution)/shard_map/reduce_scatter | solution.py:288
  1547.5 51.8 %reduce-scatter.11.cloned.1.call-done = bf16[96,2304]{1,0:T(8,128)(2,1)} async-done(((bf16[768,2304]{1,0:T(8,128)(2,1)}), bf16[96,2304]{1,0:T(8,128)(2,1)}) %reduce-scatter.11.cloned.1.call-update) | async-done | bytes 442384 | tf_op jit(solution)/shard_map/reduce_scatter | solution.py:270
  1607.7 6.7 fusion.34
  1614.4 22.4 %reduce-scatter.19.cloned.1.call-done = bf16[96,2]{1,0:T(8,128)(2,1)} async-done(((bf16[768,2]{1,0:T(8,128)(2,1)}), bf16[96,2]{1,0:T(8,128)(2,1)}) %reduce-scatter.19.cloned.1.call-update) | async-done | bytes 400
  1637.6 12.7 all-reduce.8
  1655.2 60.9 %all-reduce.12.cloned.1.call-done = (bf16[96,2304]{1,0:T(8,128)(2,1)}, bf16[96,768]{1,0:T(8,128)(2,1)}, bf16[96,3072]{1,0:T(8,128)(2,1)}, bf16[384,768]{1,0:T(8,128)(2,1)}) async-done(((bf16[96,2304]{1,0:T(8,128)(2,1)}, bf16[96,768]{1,0:T(8,128)(2,1)}, bf16[96,3072]{1,0:T(8,128)(2,1)}, bf16[384,768]{1,0:T(8,128)(2,1)}), (bf16[96,2304]{1,0:T(8,128)(2,1)}, bf16[96,768]{1,0:T(8,128)(2,1)}, ...) | async-done | bytes 1769488 | tf_op jit(solution)/shard_map/psum | solution.py:308
  (436 shorter events, 481.2 us)
Async XLA Ops:
  7.2 11.6 copy-start
  7.2 181.6 %all-gather.2.cloned.1.call-start = ((), (), s32[]{:S(2)}) async-start(), calls=%async_computation.6 | async-start | bytes 36274176 | tf_op jit(solution)/shard_map/all_gather | solution.py:133
  10.9 14.7 copy-start.20
  17.4 8.3 copy-start.29
  17.4 8.3 copy-start.24
  30.7 1360.9 %reduce-scatter.9.cloned.1.call-start = ((), (), s32[]{:S(2)}) async-start(), calls=%async_computation.7 | async-start | bytes 72548352 | tf_op jit(solution)/shard_map/reduce_scatter | solution.py:252
  359.1 47.1 %copy-start.9 = (f32[1312,768]{1,0:T(8,128)}, f32[1312,768]{1,0:T(8,128)S(1)}, u32[]{:S(2)}) copy-start(f32[1312,768]{1,0:T(8,128)S(1)} %get-tuple-element.504) | copy-start | bytes 12091396
  359.2 82.8 %copy-start.31 = (f32[1312]{0:T(1024)}, f32[1312]{0:T(1024)S(1)}, u32[]{:S(2)}) copy-start(f32[1312]{0:T(1024)S(1)} %broadcast_multiply_fusion.1) | copy-start | bytes 15748
  359.8 46.5 %copy-start.35 = (f32[1312]{0:T(1024)}, f32[1312]{0:T(1024)S(1)}, u32[]{:S(2)}) copy-start(f32[1312]{0:T(1024)S(1)} %fusion.60) | copy-start | bytes 15748
  360.4 45.9 %copy-start.22 = (f32[1312]{0:T(1024)S(1)}, f32[1312]{0:T(1024)}, u32[]{:S(2)}) copy-start(f32[1312]{0:T(1024)} %convert_element_type.232) | copy-start | bytes 15748
  427.8 14.1 copy-start.28
  427.8 14.2 copy-start.10
  427.8 14.2 copy-start.36
  427.8 14.2 copy-start.40
  451.1 21.7 %copy-start.15 = (f32[1312]{0:T(1024)S(1)}, f32[1312]{0:T(1024)}, u32[]{:S(2)}) copy-start(f32[1312]{0:T(1024)} %get-tuple-element.731) | copy-start | bytes 15748
  487.7 18.7 %copy-start.2 = (bf16[1312,8,128]{0,2,1:T(8,128)(2,1)}, bf16[1312,8,128]{0,2,1:T(8,128)(2,1)S(1)}, u32[]{:S(2)}) copy-start(bf16[1312,8,128]{0,2,1:T(8,128)(2,1)S(1)} %get-tuple-element.610) | copy-start | bytes 8060932 | tf_op jit(solution)/shard_map/while
  487.7 7.7 copy-start.4
  506.5 14.0 copy-start.1
  537.3 9.7 slice-start
  567.5 18.7 %copy-start.2 = (bf16[1312,8,128]{0,2,1:T(8,128)(2,1)}, bf16[1312,8,128]{0,2,1:T(8,128)(2,1)S(1)}, u32[]{:S(2)}) copy-start(bf16[1312,8,128]{0,2,1:T(8,128)(2,1)S(1)} %get-tuple-element.610) | copy-start | bytes 8060932 | tf_op jit(solution)/shard_map/while
  567.5 7.7 copy-start.4
  586.2 14.0 copy-start.1
  617.1 9.8 slice-start
  647.3 18.7 %copy-start.2 = (bf16[1312,8,128]{0,2,1:T(8,128)(2,1)}, bf16[1312,8,128]{0,2,1:T(8,128)(2,1)S(1)}, u32[]{:S(2)}) copy-start(bf16[1312,8,128]{0,2,1:T(8,128)(2,1)S(1)} %get-tuple-element.610) | copy-start | bytes 8060932 | tf_op jit(solution)/shard_map/while
  647.3 7.7 copy-start.4
  666.0 14.0 copy-start.1
  696.9 9.7 slice-start
  727.0 18.7 %copy-start.2 = (bf16[1312,8,128]{0,2,1:T(8,128)(2,1)}, bf16[1312,8,128]{0,2,1:T(8,128)(2,1)S(1)}, u32[]{:S(2)}) copy-start(bf16[1312,8,128]{0,2,1:T(8,128)(2,1)S(1)} %get-tuple-element.610) | copy-start | bytes 8060932 | tf_op jit(solution)/shard_map/while
  727.0 7.7 copy-start.4
  745.8 14.0 copy-start.1
  776.6 9.7 slice-start
  806.7 18.7 %copy-start.2 = (bf16[1312,8,128]{0,2,1:T(8,128)(2,1)}, bf16[1312,8,128]{0,2,1:T(8,128)(2,1)S(1)}, u32[]{:S(2)}) copy-start(bf16[1312,8,128]{0,2,1:T(8,128)(2,1)S(1)} %get-tuple-element.610) | copy-start | bytes 8060932 | tf_op jit(solution)/shard_map/while
  806.7 7.7 copy-start.4
  825.5 14.0 copy-start.1
  856.3 9.7 slice-start
  886.4 18.7 %copy-start.2 = (bf16[1312,8,128]{0,2,1:T(8,128)(2,1)}, bf16[1312,8,128]{0,2,1:T(8,128)(2,1)S(1)}, u32[]{:S(2)}) copy-start(bf16[1312,8,128]{0,2,1:T(8,128)(2,1)S(1)} %get-tuple-element.610) | copy-start | bytes 8060932 | tf_op jit(solution)/shard_map/while
  886.4 7.7 copy-start.4
  905.1 14.0 copy-start.1
  936.0 9.8 slice-start
  1019.4 455.2 %reduce-scatter.13.cloned.1.call-start = ((), (), s32[]{:S(2)}) async-start(), calls=%async_computation.9 | async-start | bytes 1327104 | tf_op jit(solution)/shard_map/reduce_scatter | solution.py:276
  1024.7 465.6 %reduce-scatter.17.cloned.1.call-start = ((), (), s32[]{:S(2)}) async-start(), calls=%async_computation.11 | async-start | bytes 5308416 | tf_op jit(solution)/shard_map/reduce_scatter | solution.py:294
  1037.4 510.0 %reduce-scatter.15.cloned.1.call-start = ((), (), s32[]{:S(2)}) async-start(), calls=%async_computation.10 | async-start | bytes 5308416 | tf_op jit(solution)/shard_map/reduce_scatter | solution.py:288
  1053.1 546.2 %reduce-scatter.11.cloned.1.call-start = ((), (), s32[]{:S(2)}) async-start(), calls=%async_computation.8 | async-start | bytes 3981312 | tf_op jit(solution)/shard_map/reduce_scatter | solution.py:270
  1057.5 340.0 %copy-start.21 = (f32[1312]{0:T(1024)S(1)}, f32[1312]{0:T(1024)}, u32[]{:S(2)}) copy-start(f32[1312]{0:T(1024)} %copy-done.20) | copy-start | bytes 15748
  1406.4 230.3 %reduce-scatter.19.cloned.1.call-start = ((), (), s32[]{:S(2)}) async-start(), calls=%async_computation.12 | async-start | bytes 221184
  1414.3 11.5 copy-start.13
  1428.3 11.0 copy-start.30
  1440.0 276.1 %all-reduce.12.cloned.1.call-start = ((), (), s32[]{:S(2)}) async-start(), calls=%async_computation.13 | async-start | bytes 3538944 | tf_op jit(solution)/shard_map/psum | solution.py:308
  (65 other events, 290.9 us)
Sparse Core Ops, SparseCore 0:
  30.8 157.9 all-gather.1
  1019.5 372.0 reduce-scatter.8
  1395.4 36.7 reduce-scatter.12
  1435.9 54.3 reduce-scatter.16
  1493.6 53.8 reduce-scatter.14
  1551.2 48.0 reduce-scatter.10
  1603.2 33.4 reduce-scatter.18
  1639.4 76.6 all-reduce.11
where the time goes:
time: 1740 us; the launch traced here: 1730 us
  waiting for transfers between devices  687 us (39%)
  matrix products  398 us (23%)
  local copies, waits for them, and re-layouts  349 us (20%)
  other arithmetic  239 us (14%)
  blocking collectives  40.3 us (2%)
    reduce_scatter x1, waiting for transfers between devices, per_device(): lax.psum_scatter(grad_memory_all, ('freq', 'tm'), scatter_dimension=0, ti...  334 us
    all_gather x1, waiting for transfers between devices, per_device(): all_memory = lax.all_gather(key_value, ('freq', 'tm'), axis=0, tiled=True)  144 us
    dynamic_update_slice x12, other arithmetic, add_lanes(): return lax.dynamic_update_slice_in_dim(target, current + addend, offset, 2)  78.9 us
    dynamic_slice x36, local copies, waits for them, and re-layouts, head_pair(): section = lax.dynamic_slice_in_dim(array, offset, lane_width, 2)  78.8 us
    dot_general x4, matrix products, matmul(): return jnp.dot(left, right, preferred_element_type=jnp.float32)  68.8 us
    while x1, local copies, waits for them, and re-layouts, per_device(): lax.fori_loop(0, pair_count, backward_pair, (zero_query, jnp.zeros((key_c...  67.9 us
    dot_general x6, matrix products, pair_probs(): jnp.einsum('qchd,kchd->chqk', query_pair, key_pair, preferred_element_typ...  66.2 us
    convert_element_type x6, other arithmetic, query_side(): grad_scores = (probability * (grad_probs - delta)).astype(jnp.bfloat16)  62.9 us
  transfers between devices with their start and end apart: 8, of which 7 were waited for; matrix products, arithmetic and copies ran while one was open for 7% of the time, Pallas kernels for 0%

commit v1 on v0

--- a/solution.py
+++ b/solution.py
@@ -9,6 +9,12 @@
 FREQ_ROWS = 12
 EPS = 1e-06
 NEG = -1000000000.0
+
+
+def add_all(x, axis):
+    parts = lax.all_gather(x, axis, axis=0, tiled=False)
+    total = parts.sum(axis=0)
+    return total
 
 
 def live_slots(col_counts, slot_ids, freq_ids, time_ids, freq_rows, cap_cols):
@@ -305,7 +311,7 @@
         ).astype(jnp.float32),
     )
     summed_all = (
-        lax.psum(shares[0].astype(jnp.bfloat16), "dp").astype(jnp.float32),
+        add_all(shares[0].astype(jnp.bfloat16), "dp").astype(jnp.float32),
         lax.psum(shares[1].astype(jnp.bfloat16), "dp").astype(jnp.float32),
         lax.psum(shares[2].astype(jnp.bfloat16), "dp").astype(jnp.float32),
         lax.psum(shares[3].astype(jnp.bfloat16), "dp").astype(jnp.float32),

time: 1740 us -> 1650 us (0.948)
  waiting for transfers between devices: 687 us -> 583 us
    reduce_scatter x1, waiting for transfers between devices: 57.2 us -> 0.01 us  [per_device(): lax.psum_scatter(grad_up_part.astype(jnp.bfloat16), ('freq', 'tm'), scatt...]
    reduce_scatter x1, waiting for transfers between devices: 334 us -> 368 us  [per_device(): lax.psum_scatter(grad_memory_all, ('freq', 'tm'), scatter_dimension=0, ti...]
    psum x1, waiting for transfers between devices: 60.9 us -> 29.7 us  [per_device(): lax.psum(shares[2].astype(jnp.bfloat16), 'dp').astype(jnp.float32)]
    unnamed x9 -> x10, waiting for transfers between devices: 22.5 us -> 0.15 us
    reduce_scatter x1, waiting for transfers between devices: 51.8 us -> 29.6 us  [per_device(): lax.psum_scatter(grad_joint_part.astype(jnp.bfloat16), ('freq', 'tm'), sc...]
  transfers between devices with their start and end apart: 8 -> 9, of which waited for: 7 -> 5; matrix products, arithmetic and copies ran while one was open for 7% -> 42% of each run, Pallas kernels for 0% -> 0%
where the time goes in v1:
time: 1650 us; the launch traced here: 1630 us
  waiting for transfers between devices  583 us (35%)
  matrix products  396 us (24%)
  local copies, waits for them, and re-layouts  354 us (21%)
  other arithmetic  243 us (15%)
  blocking collectives  40.1 us (2%)
    reduce_scatter x1, waiting for transfers between devices, per_device(): lax.psum_scatter(grad_memory_all, ('freq', 'tm'), scatter_dimension=0, ti...  368 us
    all_gather x1, waiting for transfers between devices, per_device(): all_memory = lax.all_gather(key_value, ('freq', 'tm'), axis=0, tiled=True)  144 us
    dynamic_update_slice x12, other arithmetic, add_lanes(): return lax.dynamic_update_slice_in_dim(target, current + addend, offset, 2)  79.1 us
    dynamic_slice x36, local copies, waits for them, and re-layouts, head_pair(): section = lax.dynamic_slice_in_dim(array, offset, lane_width, 2)  79.1 us
    dot_general x4, matrix products, matmul(): return jnp.dot(left, right, preferred_element_type=jnp.float32)  68.5 us
    while x1, local copies, waits for them, and re-layouts, per_device(): lax.fori_loop(0, pair_count, backward_pair, (zero_query, jnp.zeros((key_c...  67.7 us
    dot_general x6, matrix products, pair_probs(): jnp.einsum('qchd,kchd->chqk', query_pair, key_pair, preferred_element_typ...  66.2 us
    convert_element_type x6, other arithmetic, query_side(): grad_scores = (probability * (grad_probs - delta)).astype(jnp.bfloat16)  63 us
  transfers between devices with their start and end apart: 9, of which 5 were waited for; matrix products, arithmetic and copies ran while one was open for 42% of the time, Pallas kernels for 0%

profile of v1, /device:TPU:0, one launch (start us, length us, event | category | flops | bytes accessed | tf_op | source)
XLA Modules:
  0.0 1634.8 jit_solution(5558651745290250847)
XLA Ops:
  18.8 6.9 fusion.65
  44.4 144.4 %all-gather.4.cloned.1.call-done = bf16[1312,8,1536]{2,1,0:T(8,128)(2,1)} async-done(((bf16[164,8,1536]{2,1,0:T(8,128)(2,1)}), bf16[1312,8,1536]{2,1,0:T(8,128)(2,1)}) %all-gather.4.cloned.1.call-update) | async-done | bytes 32243728 | tf_op jit(solution)/shard_map/all_gather | solution.py:139
  188.8 42.4 %copy.42 = bf16[1312,8,1536]{0,2,1:T(8,128)(2,1)} copy(bf16[1312,8,1536]{2,1,0:T(8,128)(2,1)} %all-gather.4.cloned.1.call-done) | data formatting | bytes 64487424 | tf_op jit(solution)/shard_map/while | solution.py:166
  231.9 122.6 %while.34 = (s32[]{:T(128)}, bf16[164,8,768]{2,1,0:T(8,128)(2,1)}, f32[164,8,12]{0,2,1:T(8,128)}, bf16[1312,8,1536]{0,2,1:T(8,128)(2,1)}, bf16[164,8,768]{0,2,1:...) while((s32[]{:T(128)}, bf16[164,8,768]{2,1,0:T(8,128)(2,1)}, ...), condition=%wide.region_6.7_spmd, body=%wide.region_3.6_spmd.sunk | while | flops 922637760 | bytes 60295916 | solution.py:166
  360.9 45.8 %multiply_convert_fusion.1 = (bf16[1312,3072]{1,0:T(8,128)(2,1)}, f32[1312,3072]{1,0:T(8,128)}, f32[1312,3072]{1,0:T(8,128)}) fusion(f32[3072]{0:T(1024)S(1)} %copy-done.42, bf16[768,3072]{1,0:T(8,128)(2,1)S(1)} %bitcast.206, f32[1312,768]{1,0:T(8,128)S(1)} %get-tuple-element.503, f32[768]{0:T(1024)S(1)} %copy-done.49, f32[768]{0:T(1024)S(1)} %copy-done.39, ...), kind=kOutput, calls=%fused_computation.34 | convolution fusion | flops 6461841408 | bytes 49082624 | tf_op jit(solution)/shard_map/dot_general | solution.py:42
  406.7 21.5 %fusion.75 = (bf16[3072]{0:T(1024)(128)(2,1)}, bf16[1312,3072]{1,0:T(8,128)(2,1)}) fusion(f32[1312,3072]{1,0:T(8,128)} %get-tuple-element.491, bf16[3072,768]{1,0:T(8,128)(2,1)} %param.25, bf16[164,8,768]{2,1,0:T(8,128)(2,1)} %param.27, f32[1312]{0:T(1024)S(1)} %copy-done.23, f32[1312,3072]{1,0:T(8,128)} %get-tuple-element.504, f32[3072]{0:T(1024)} %convert_element_type.231), kind=kOutput, calls=%fused_computation.178 | convolution fusion | flops 6258299904 | bytes 47062144 | tf_op jit(solution)/shard_map/dot_general | solution.py:52
  428.2 14.1 multiply_reduce_fusion.1
  450.4 12.5 convolution_convert_fusion.2
  468.1 13.2 convolution_convert_fusion.1
  483.6 23.7 %broadcast_in_dim.96 = f32[1312,8,1536]{0,2,1:T(8,128)} broadcast(f32[]{:T(128)} %constant.302.clone.1), dimensions={} | broadcast | bytes 64487428 | tf_op jit(solution)/shard_map/broadcast_in_dim | solution.py:256
  507.3 480.6 %while.35 = (s32[]{:T(128)}, f32[164,8,768]{2,1,0:T(8,128)}, f32[1312,8,1536]{0,2,1:T(8,128)}, bf16[1312,8,1536]{0,2,1:T(8,128)(2,1)}, bf16[164,8,768]{0,2,1:T(8...) while((s32[]{:T(128)}, f32[164,8,768]{2,1,0:T(8,128)}, ...), condition=%wide.region_14.15_spmd, body=%wide.region_12.14_spmd.sunk | while | flops 2238668288 | bytes 267073456 | solution.py:252
  522.7 7.6 fusion.137
  530.4 11.0 multiply_reduce_fusion.5
  541.4 10.6 multiply_convert_fusion.4
  575.7 7.6 constant_dynamic-update-slice_fusion.10
  583.4 5.8 constant_dynamic-update-slice_fusion.11
  604.0 7.6 fusion.137
  611.7 11.0 multiply_reduce_fusion.5
  622.7 10.5 multiply_convert_fusion.4
  655.8 7.5 constant_dynamic-update-slice_fusion.10
  663.4 5.7 constant_dynamic-update-slice_fusion.11
  683.9 7.6 fusion.137
  691.5 11.0 multiply_reduce_fusion.5
  702.6 10.5 multiply_convert_fusion.4
  735.6 7.5 constant_dynamic-update-slice_fusion.10
  763.5 7.6 fusion.137
  771.2 11.0 multiply_reduce_fusion.5
  782.3 10.5 multiply_convert_fusion.4
  815.3 7.5 constant_dynamic-update-slice_fusion.10
  843.2 7.6 fusion.137
  850.8 11.0 multiply_reduce_fusion.5
  861.9 10.5 multiply_convert_fusion.4
  895.0 7.5 constant_dynamic-update-slice_fusion.10
  922.9 7.6 fusion.137
  930.6 11.0 multiply_reduce_fusion.5
  941.6 10.5 multiply_convert_fusion.4
  974.8 7.5 constant_dynamic-update-slice_fusion.10
  987.9 67.7 %copy.49 = f32[1312,8,1536]{2,1,0:T(8,128)} copy(f32[1312,8,1536]{0,2,1:T(8,128)} %get-tuple-element.368) | data formatting | bytes 128974848 | tf_op jit(solution)/shard_map/while | solution.py:252
  1059.4 368.3 %reduce-scatter.9.cloned.1.call-done = f32[164,8,1536]{2,1,0:T(8,128)} async-done(((f32[1312,8,1536]{2,1,0:T(8,128)}), f32[164,8,1536]{2,1,0:T(8,128)}) %reduce-scatter.9.cloned.1.call-update) | async-done | bytes 8060944 | tf_op jit(solution)/shard_map/reduce_scatter | solution.py:258
  1433.7 8.8 convolution_convert_fusion
  1451.1 11.2 fusion.40
  1462.3 29.7 %all-reduce.12.cloned.1.call-done = (bf16[96,768]{1,0:T(8,128)(2,1)}, bf16[96,3072]{1,0:T(8,128)(2,1)}, bf16[384,768]{1,0:T(8,128)(2,1)}) async-done(((bf16[96,768]{1,0:T(8,128)(2,1)}, bf16[96,3072]{1,0:T(8,128)(2,1)}, bf16[384,768]{1,0:T(8,128)(2,1)}), (bf16[96,768]{1,0:T(8,128)(2,1)}, bf16[96,3072]{1,0:T(8,128)(2,1)}, bf16[384,768]{1,0:T(8,128)(2,1)})) %all-reduce.12.cloned.1.call-update) | async-done | bytes 1327120 | tf_op jit(solution)/shard_map/psum | solution.py:316
  1502.3 11.7 fusion.69
  1514.0 29.6 %reduce-scatter.11.cloned.1.call-done = bf16[96,2304]{1,0:T(8,128)(2,1)} async-done(((bf16[768,2304]{1,0:T(8,128)(2,1)}), bf16[96,2304]{1,0:T(8,128)(2,1)}) %reduce-scatter.11.cloned.1.call-update) | async-done | bytes 442384 | tf_op jit(solution)/shard_map/reduce_scatter | solution.py:276
  1550.0 27.0 %all-reduce.7 = (bf16[768]{0:T(1024)(128)(2,1)}, bf16[768]{0:T(1024)(128)(2,1)}, bf16[768]{0:T(1024)(128)(2,1)}, bf16[768]{0:T(1024)(128)(2,1)}, bf16[3072]{0:T(...) all-reduce(bf16[768]{0:T(1024)(128)(2,1)} %get-tuple-element.425, ...), channel_id=5, replica_groups=mesh['dp'=4,'freq'=2,'tm'=4] {'freq','tm'}, use_global_device_ids=true, to_apply=%region_22.23.clone | all-reduce | flops 7680 | bytes 30720
  1586.6 6.9 fusion.34
  1594.4 13.1 all-reduce.8
  1612.3 11.2 all-gather.6.cloned.1.call-done
  (444 shorter events, 476.3 us)
Async XLA Ops:
  7.2 11.6 copy-start
  7.2 181.6 %all-gather.4.cloned.1.call-start = ((), (), s32[]{:S(2)}) async-start(), calls=%async_computation.6 | async-start | bytes 36274176 | tf_op jit(solution)/shard_map/all_gather | solution.py:139
  10.9 14.7 copy-start.21
  17.4 8.3 copy-start.31
  17.4 8.3 copy-start.26
  30.7 1028.6 %reduce-scatter.13.cloned.1.call-start = ((), (), s32[]{:S(2)}) async-start(), calls=%async_computation.9 | async-start | bytes 1327104 | tf_op jit(solution)/shard_map/reduce_scatter | solution.py:282
  359.1 47.6 %copy-start.9 = (f32[1312,768]{1,0:T(8,128)}, f32[1312,768]{1,0:T(8,128)S(1)}, u32[]{:S(2)}) copy-start(f32[1312,768]{1,0:T(8,128)S(1)} %get-tuple-element.503) | copy-start | bytes 12091396
  359.8 46.9 %copy-start.34 = (f32[1312]{0:T(1024)}, f32[1312]{0:T(1024)S(1)}, u32[]{:S(2)}) copy-start(f32[1312]{0:T(1024)S(1)} %fusion.60) | copy-start | bytes 15748
  360.8 45.9 %copy-start.23 = (f32[1312]{0:T(1024)S(1)}, f32[1312]{0:T(1024)}, u32[]{:S(2)}) copy-start(f32[1312]{0:T(1024)} %convert_element_type.234) | copy-start | bytes 15748
  428.2 14.1 copy-start.30
  428.2 14.1 copy-start.10
  428.2 14.2 copy-start.35
  428.2 14.2 copy-start.40
  450.4 608.9 %reduce-scatter.17.cloned.1.call-start = ((), (), s32[]{:S(2)}) async-start(), calls=%async_computation.11 | async-start | bytes 5308416 | tf_op jit(solution)/shard_map/reduce_scatter | solution.py:300
  462.9 596.4 %reduce-scatter.15.cloned.1.call-start = ((), (), s32[]{:S(2)}) async-start(), calls=%async_computation.10 | async-start | bytes 5308416 | tf_op jit(solution)/shard_map/reduce_scatter | solution.py:294
  481.3 946.4 %reduce-scatter.9.cloned.1.call-start = ((), (), s32[]{:S(2)}) async-start(), calls=%async_computation.7 | async-start | bytes 72548352 | tf_op jit(solution)/shard_map/reduce_scatter | solution.py:258
  483.6 23.7 %copy-start.15 = (f32[1312]{0:T(1024)S(1)}, f32[1312]{0:T(1024)}, u32[]{:S(2)}) copy-start(f32[1312]{0:T(1024)} %get-tuple-element.729) | copy-start | bytes 15748
  522.7 18.7 %copy-start.2 = (bf16[1312,8,128]{0,2,1:T(8,128)(2,1)}, bf16[1312,8,128]{0,2,1:T(8,128)(2,1)S(1)}, u32[]{:S(2)}) copy-start(bf16[1312,8,128]{0,2,1:T(8,128)(2,1)S(1)} %get-tuple-element.609) | copy-start | bytes 8060932 | tf_op jit(solution)/shard_map/while
  522.7 7.7 copy-start.4
  541.4 14.6 copy-start.1
  573.5 9.9 slice-start
  604.0 18.7 %copy-start.2 = (bf16[1312,8,128]{0,2,1:T(8,128)(2,1)}, bf16[1312,8,128]{0,2,1:T(8,128)(2,1)S(1)}, u32[]{:S(2)}) copy-start(bf16[1312,8,128]{0,2,1:T(8,128)(2,1)S(1)} %get-tuple-element.609) | copy-start | bytes 8060932 | tf_op jit(solution)/shard_map/while
  604.0 7.7 copy-start.4
  622.7 14.0 copy-start.1
  653.6 9.8 slice-start
  683.8 18.7 %copy-start.2 = (bf16[1312,8,128]{0,2,1:T(8,128)(2,1)}, bf16[1312,8,128]{0,2,1:T(8,128)(2,1)S(1)}, u32[]{:S(2)}) copy-start(bf16[1312,8,128]{0,2,1:T(8,128)(2,1)S(1)} %get-tuple-element.609) | copy-start | bytes 8060932 | tf_op jit(solution)/shard_map/while
  683.9 7.7 copy-start.4
  702.6 14.0 copy-start.1
  733.5 9.7 slice-start
  763.5 18.7 %copy-start.2 = (bf16[1312,8,128]{0,2,1:T(8,128)(2,1)}, bf16[1312,8,128]{0,2,1:T(8,128)(2,1)S(1)}, u32[]{:S(2)}) copy-start(bf16[1312,8,128]{0,2,1:T(8,128)(2,1)S(1)} %get-tuple-element.609) | copy-start | bytes 8060932 | tf_op jit(solution)/shard_map/while
  763.5 7.7 copy-start.4
  782.2 14.0 copy-start.1
  813.1 9.6 slice-start
  843.1 18.7 %copy-start.2 = (bf16[1312,8,128]{0,2,1:T(8,128)(2,1)}, bf16[1312,8,128]{0,2,1:T(8,128)(2,1)S(1)}, u32[]{:S(2)}) copy-start(bf16[1312,8,128]{0,2,1:T(8,128)(2,1)S(1)} %get-tuple-element.609) | copy-start | bytes 8060932 | tf_op jit(solution)/shard_map/while
  843.2 7.7 copy-start.4
  861.9 14.0 copy-start.1
  892.8 9.7 slice-start
  922.9 18.7 %copy-start.2 = (bf16[1312,8,128]{0,2,1:T(8,128)(2,1)}, bf16[1312,8,128]{0,2,1:T(8,128)(2,1)S(1)}, u32[]{:S(2)}) copy-start(bf16[1312,8,128]{0,2,1:T(8,128)(2,1)S(1)} %get-tuple-element.609) | copy-start | bytes 8060932 | tf_op jit(solution)/shard_map/while
  941.6 14.0 copy-start.1
  972.5 9.8 slice-start
  1055.6 436.3 %all-reduce.12.cloned.1.call-start = ((), (), s32[]{:S(2)}) async-start(), calls=%async_computation.14 | async-start | bytes 2654208 | tf_op jit(solution)/shard_map/psum | solution.py:316
  1059.4 374.3 %copy-start.22 = (f32[1312]{0:T(1024)S(1)}, f32[1312]{0:T(1024)}, u32[]{:S(2)}) copy-start(f32[1312]{0:T(1024)} %copy-done.21) | copy-start | bytes 15748
  1059.4 374.3 %copy-start.27 = (f32[1312]{0:T(1024)S(1)}, f32[1312]{0:T(1024)}, u32[]{:S(2)}) copy-start(f32[1312]{0:T(1024)} %copy-done.26) | copy-start | bytes 15748
  1059.4 484.2 %reduce-scatter.11.cloned.1.call-start = ((), (), s32[]{:S(2)}) async-start(), calls=%async_computation.8 | async-start | bytes 3981312 | tf_op jit(solution)/shard_map/reduce_scatter | solution.py:276
  1442.6 8.5 copy-start.24
  1442.6 151.0 %reduce-scatter.19.cloned.1.call-start = ((), (), s32[]{:S(2)}) async-start(), calls=%async_computation.13 | async-start | bytes 221184
  1491.9 7.9 copy-start.43
  1502.0 121.5 %all-gather.6.cloned.1.call-start = ((), (), s32[]{:S(2)}) async-start(), calls=%async_computation.12 | async-start | bytes 2211840 | tf_op jit(solution)/shard_map/all_gather | solution.py:15
  (68 other events, 311.7 us)
Sparse Core Ops, SparseCore 0:
  30.8 157.9 all-gather.3
  450.5 36.7 reduce-scatter.12
  491.1 53.8 reduce-scatter.16
  548.4 53.8 reduce-scatter.14
  1055.8 371.9 reduce-scatter.8
  1430.3 61.5 all-reduce.11
  1495.8 47.7 reduce-scatter.10
  1547.5 33.4 reduce-scatter.18
  1582.6 40.8 all-gather.5
